TPU v7x, 32 devices: a whole 2x2x4 slice. The times are simulated.
32 devices in a mesh: groups: 2 (over x), seq: 16 (over z, y, core).
Axes of the slice: x: 2, y: 2, z: 4, core: 2. Of those that a mesh axis runs over, the one named last changes fastest.
Arguments:
- queries: bfloat16 [8192, 2048], P(('groups', 'seq')), parts along dimension 0, may hold values from -400 to 400
- neighbours: bfloat16 [64, 128, 896], P(('groups', 'seq')), parts along dimension 0, may hold values from -500 to 500
- w_key: bfloat16 [896, 2048], replicated, may hold values from -0.1875 to 0.1875
- w_value: bfloat16 [896, 2048], replicated, may hold values from -0.1875 to 0.1875
- retrieval_owner: int32 [128, 2], P(('groups', 'seq')), parts along dimension 0, may hold values from 0 to 15, as said below
- retrieval_slot: int32 [128, 2], P(('groups', 'seq')), parts along dimension 0, may hold values from 0 to 1
- doc_starts: int32 [128], P(('groups', 'seq')), parts along dimension 0, may hold values 0 or 1
Outputs:
- attended: bfloat16 [8192, 2048], P(('groups', 'seq')), parts along dimension 0
There are 2 independent parts, one for each index of `groups`. A program takes and returns all parts, laid end to end along the dimension named above; an argument that names none is the same for every part. Nothing has to cross between parts.
Inputs may be any that keep to these rules, and one draw needn't show every extreme that they name: `retrieval_owner`: among the 8 owners named by the spans of one device, no owner appears more than 1 times, and some owner appears exactly 1 times.
All inputs are finite; a program needn't handle non-finite values. No bound on the sum of `doc_starts` on one device may be relied on, other than what follows from the above.
Results may differ from a plain program's by a relative error of at most 0.0071.
Values may be sent and summed in bfloat16 or wider, within the bound.
A program may use at most 128 MiB of HBM per device.

v0:
```python
import math

import jax
import jax.numpy as jnp
from jax import lax
from jax.sharding import PartitionSpec as P

SPAN = 64
HEADS = 16
HEAD_DIM = 128


def from_behind(value, axis, steps):
    count = lax.axis_size(axis)
    first, last = (max(0, -steps), min(count, count - steps))
    return lax.ppermute(value, axis, [(source, source + steps) for source in range(first, last)])


def normalize(tokens_in):
    widened = tokens_in.astype(jnp.float32)
    factor = lax.rsqrt(jnp.mean(widened * widened, axis=-1, keepdims=True) + 1e-06)
    return (widened * factor).astype(jnp.bfloat16)


def ranks_of(owner_rows):
    count = owner_rows.shape[-1]
    same = owner_rows[..., :, None] == owner_rows[..., None, :]
    earlier = jnp.arange(count)[:, None] > jnp.arange(count)[None, :]
    return jnp.sum(jnp.where(same & earlier, 1, 0), axis=-1).astype(jnp.int32)


def project(chosen, w_key, w_value, span_count):
    model_width = w_key.shape[1]
    normed = normalize(chosen).reshape(-1, chosen.shape[-1])
    key_rows = jnp.dot(normed, w_key, preferred_element_type=jnp.float32).astype(jnp.bfloat16)
    value_rows = jnp.dot(normed, w_value, preferred_element_type=jnp.float32).astype(jnp.bfloat16)
    return (
        key_rows.reshape(span_count, -1, model_width),
        value_rows.reshape(span_count, -1, model_width),
    )


def attend(query_rows, key_rows, value_rows):
    windows = query_rows.shape[0]
    query_heads = query_rows.reshape(windows, SPAN, HEADS, HEAD_DIM)
    key_heads = key_rows.reshape(windows, -1, HEADS, HEAD_DIM)
    value_heads = value_rows.reshape(windows, -1, HEADS, HEAD_DIM)
    scores = jnp.einsum(
        "wqhd,wkhd->whqk", query_heads, key_heads, preferred_element_type=jnp.float32
    )
    scores = scores * (1.0 / math.sqrt(HEAD_DIM))
    highest = jnp.max(scores, axis=-1, keepdims=True)
    powers = jnp.exp(scores - highest)
    totals = jnp.sum(powers, axis=-1, keepdims=True)
    weights = (powers / totals).astype(jnp.bfloat16)
    result = jnp.einsum("whqk,wkhd->wqhd", weights, value_heads, preferred_element_type=jnp.float32)
    return result.reshape(windows * SPAN, HEADS * HEAD_DIM).astype(jnp.bfloat16)


def body(queries, neighbours, w_key, w_value, retrieval_owner, retrieval_slot, doc_starts):
    peer_count = lax.axis_size("seq")
    span_count = doc_starts.shape[0]
    token_count = queries.shape[0]
    model_width = queries.shape[1]
    request_count = 2 * span_count
    capacity = (request_count + peer_count - 1) // peer_count
    owners = retrieval_owner.reshape(-1)
    slot_ids = retrieval_slot.reshape(-1)
    destination = owners * capacity + ranks_of(owners)
    targets = jnp.arange(peer_count * capacity, dtype=jnp.int32)
    matches = destination[:, None] == targets[None, :]
    wanted = jnp.sum(jnp.where(matches, slot_ids[:, None] + 1, 0), axis=0) - 1
    asked_slot = lax.all_to_all(
        wanted.reshape(peer_count, capacity), "seq", split_axis=0, concat_axis=0, tiled=True
    ).reshape(-1)
    picked = jnp.take(neighbours, jnp.maximum(asked_slot, 0), axis=0)
    incoming = lax.all_to_all(picked, "seq", split_axis=0, concat_axis=0, tiled=True)
    chosen = jnp.take(incoming, destination, axis=0)
    key_rows, value_rows = project(chosen, w_key, w_value, span_count)
    tail_rows = from_behind(queries[: SPAN - 1], "seq", -1)
    query_rows = jnp.concatenate([queries[SPAN - 1 :], tail_rows], 0).reshape(
        span_count, SPAN, model_width
    )
    computed = attend(query_rows, key_rows, value_rows)
    head_rows = from_behind(computed[token_count - SPAN + 1 :], "seq", 1)
    attended = jnp.concatenate([head_rows, computed[: token_count - SPAN + 1]], 0)
    offsets = jnp.arange(SPAN)
    fresh_rows = (doc_starts[:, None] == 0) | (offsets[None, :] == SPAN - 1)
    opening = (
        (lax.axis_index("seq") == 0)
        & (jnp.arange(span_count)[:, None] == 0)
        & (offsets[None, :] < SPAN - 1)
    )
    kept_rows = (fresh_rows & jnp.logical_not(opening)).reshape(token_count)
    return jnp.where(kept_rows[:, None], attended, jnp.zeros((), jnp.bfloat16))


def solution(mesh):
    return jax.shard_map(
        body,
        mesh=mesh,
        in_specs=(
            P(("groups", "seq"), None),
            P(("groups", "seq"), None, None),
            P(),
            P(),
            P(("groups", "seq"), None),
            P(("groups", "seq"), None),
            P(("groups", "seq")),
        ),
        out_specs=P(("groups", "seq"), None),
        check_vma=False,
    )
```

profile of v0, /device:TPU:18, one launch (start us, length us, event | category | flops | bytes accessed | tf_op | source)
XLA Modules:
  0.0 157.6 jit_solution(7107284511529906446)
XLA Ops:
  0.0 0.8 copy.36
  0.9 0.2 select_reduce_fusion.1
  1.1 0.7 broadcast_add_fusion
  2.2 10.1 %all_to_all.11 = s32[16,1,1]{2,1,0:T(1,128)S(1)} all-to-all(s32[16,1,1]{2,1,0:T(1,128)S(1)} %copy.38), channel_id=1, replica_groups=mesh['groups'=2,'seq'=16] {'seq'}, dimensions={0} | all-to-all | bytes 128 | tf_op jit(solution)/shard_map/all_to_all | solution.py:73
  12.2 0.4 maximum_reduce_fusion
  12.6 2.8 %gather_fusion = bf16[16,128,896]{2,1,0:T(8,128)(2,1)} fusion(bf16[2,128,896]{2,1,0:T(8,128)(2,1)S(1)} %copy-done, s32[1024]{0:T(1024)S(1)} %pad_clamp_fusion.1), kind=kCustom, calls=%fused_computation | custom fusion | bytes 7340096 | tf_op jit(solution)/shard_map/jit(_take)/gather | solution.py:76
  15.4 0.4 compare_reduce_fusion
  15.8 4.3 %broadcast_select_fusion = bf16[16,128,896]{2,1,0:T(8,128)(2,1)} fusion(bf16[16,128,896]{2,1,0:T(8,128)(2,1)} %gather_fusion, pred[16]{0:T(512)(128)(4,1)S(1)} %compare_reduce_fusion), kind=kLoop, calls=%fused_computation.15 | loop fusion | flops 1835008 | bytes 7340048 | tf_op jit(solution)/shard_map/jit(_take)/select_n | solution.py:76
  20.1 6.8 %all-to-all-start.1 = ((bf16[16,128,896]{2,1,0:T(8,128)(2,1)}), bf16[16,128,896]{2,1,0:T(8,128)(2,1)}, u32[]{:S(2)}, u32[]{:S(2)}) async-start(bf16[16,128,896]{2,1,0:T(8,128)(2,1)} %broadcast_select_fusion), calls=%async_computation.1 | async-start | bytes 7340032 | tf_op jit(solution)/shard_map/all_to_all | solution.py:77
  27.0 3.1 %collective-permute-start = (bf16[63,2048]{1,0:T(8,128)(2,1)S(1)}, bf16[63,2048]{1,0:T(8,128)(2,1)S(1)}, u32[]{:S(2)}, u32[]{:S(2)}) collective-permute-start(bf16[63,2048]{1,0:T(8,128)(2,1)S(1)} %slice.13), channel_id=1, source_target_pairs={{1,0},{2,1},{3,2},{4,3},{5,4},{6,5},{7,6},{8,7},{9,8},{10,9},{11,1... | collective-permute-start | bytes 774152 | tf_op jit(solution)/shard_map/ppermute | solution.py:16
  30.3 0.2 slice.12
  30.5 78.8 %collective-permute-done = bf16[63,2048]{1,0:T(8,128)(2,1)S(1)} collective-permute-done((bf16[63,2048]{1,0:T(8,128)(2,1)S(1)}, bf16[63,2048]{1,0:T(8,128)(2,1)S(1)}, u32[]{:S(2)}, u32[]{:S(2)}) %collective-permute-start) | collective-permute-done | bytes 258080 | tf_op jit(solution)/shard_map/ppermute | solution.py:16
  109.3 0.1 maximum_bitcast_fusion
  109.4 0.2 copy.44
  109.6 2.9 %gather_fusion.1 = bf16[8,128,896]{2,1,0:T(8,128)(2,1)S(1)} fusion(bf16[16,128,896]{2,1,0:T(8,128)(2,1)} %all-to-all-done.1, s32[1024]{0:T(1024)S(1)} %pad_clamp_fusion), kind=kCustom, calls=%fused_computation.1 | custom fusion | bytes 3670048 | tf_op jit(solution)/shard_map/jit(_take)/gather | solution.py:78
  112.6 0.6 multiply_reduce_fusion.1
  113.2 0.5 multiply_convert_fusion
  113.7 0.9 copy-done.4
  114.6 4.7 %convert_bitcast_fusion = bf16[128,8,16,128]{3,1,2,0:T(8,128)(2,1)S(1)} fusion(bf16[1024,896]{1,0:T(8,128)(2,1)S(1)} %multiply_convert_fusion, bf16[896,2048]{1,0:T(8,128)(2,1)S(1)} %copy-done.4), kind=kOutput, calls=%fused_computation.9 | convolution fusion | flops 3760193536 | bytes 9699328 | tf_op jit(solution)/shard_map/dot_general | solution.py:35
  119.3 1.4 copy.45
  120.7 1.6 %fusion.3 = f32[4,16,64,256]{3,2,1,0:T(8,128)S(1)} fusion(bf16[4,256,16,128]{3,2,1,0:T(8,128)(2,1)S(1)} %bitcast.39, bf16[4,64,16,128]{3,2,1,0:T(8,128)(2,1)S(1)} %bitcast.42), kind=kOutput, calls=%fused_computation.5 | convolution fusion | flops 268435456 | bytes 9437184 | tf_op jit(solution)/shard_map/wqhd,wkhd->whqk/dot_general | solution.py:48
  122.3 2.0 %copy-done.1 = f32[4,16,64,256]{3,2,1,0:T(8,128)} copy-done((f32[4,16,64,256]{3,2,1,0:T(8,128)}, f32[4,16,64,256]{3,2,1,0:T(8,128)S(1)}, u32[]{:S(2)}) %copy-start.1) | copy-done | bytes 4194328
  124.3 1.6 %fusion.27 = f32[4,16,64]{2,1,0:T(8,128)S(1)} fusion(f32[4,16,64,256]{3,2,1,0:T(8,128)S(1)} %fusion.3), kind=kOutput, calls=%fused_computation.51 | output fusion | flops 4194559 | bytes 4210688 | tf_op jit(solution)/shard_map/sub | solution.py:53
  125.9 0.5 copy-done.5
  126.3 4.9 %convert_bitcast_fusion.1 = bf16[128,8,16,128]{3,1,2,0:T(8,128)(2,1)S(1)} fusion(bf16[1024,896]{1,0:T(8,128)(2,1)S(1)} %multiply_convert_fusion, bf16[896,2048]{1,0:T(8,128)(2,1)S(1)} %copy-done.5), kind=kOutput, calls=%fused_computation.10 | convolution fusion | flops 3760193536 | bytes 9699328 | tf_op jit(solution)/shard_map/dot_general | solution.py:36
  131.2 3.3 %copy.46 = bf16[128,8,16,128]{3,2,1,0:T(8,128)(2,1)} copy(bf16[128,8,16,128]{3,1,2,0:T(8,128)(2,1)S(1)} %convert_bitcast_fusion.1) | data formatting | bytes 8388608
  134.5 11.9 %fusion.13 = bf16[4,64,16,128]{3,1,2,0:T(8,128)(2,1)S(1)} fusion(bf16[4,256,16,128]{3,2,1,0:T(8,128)(2,1)} %bitcast.43, f32[4,16,64]{2,1,0:T(8,128)S(1)} %fusion.27, f32[4,16,64,256]{3,2,1,0:T(8,128)} %copy-done.1), kind=kOutput, calls=%fused_computation.20 | convolution fusion | flops 274206976 | bytes 9453568 | tf_op jit(solution)/shard_map/whqk,wkhd->wqhd/dot_general | solution.py:56
  146.5 0.7 copy.43
  147.2 0.3 copy.59
  147.5 1.9 %collective-permute-start.1 = (bf16[63,2048]{1,0:T(8,128)(2,1)S(1)}, bf16[63,2048]{1,0:T(8,128)(2,1)S(1)}, u32[]{:S(2)}, u32[]{:S(2)}) collective-permute-start(bf16[63,2048]{1,0:T(8,128)(2,1)S(1)} %slice.20), channel_id=1, source_target_pairs={{0,1},{1,2},{2,3},{3,4},{4,5},{5,6},{6,7},{7,8},{8,9},{9,10},{10,1... | collective-permute-start | bytes 774152 | tf_op jit(solution)/shard_map/ppermute | solution.py:16
  149.7 6.6 %collective-permute-done.1 = bf16[63,2048]{1,0:T(8,128)(2,1)S(1)} collective-permute-done((bf16[63,2048]{1,0:T(8,128)(2,1)S(1)}, bf16[63,2048]{1,0:T(8,128)(2,1)S(1)}, u32[]{:S(2)}, u32[]{:S(2)}) %collective-permute-start.1) | collective-permute-done | bytes 258080 | tf_op jit(solution)/shard_map/ppermute | solution.py:16
  156.3 1.3 maximum_select_fusion
  (30 shorter events, 1.0 us)
Async XLA Ops:
  0.0 12.6 %copy-start = (bf16[2,128,896]{2,1,0:T(8,128)(2,1)S(1)}, bf16[2,128,896]{2,1,0:T(8,128)(2,1)}, u32[]{:S(2)}) copy-start(bf16[2,128,896]{2,1,0:T(8,128)(2,1)} %param.8) | copy-start | bytes 1376260
  20.1 6.8 %copy-start.2 = (bf16[256,2048]{1,0:T(8,128)(2,1)S(1)}, bf16[256,2048]{1,0:T(8,128)(2,1)}, u32[]{:S(2)}) copy-start(bf16[256,2048]{1,0:T(8,128)(2,1)} %param.7) | copy-start | bytes 3145732
  20.1 10.3 %copy-start.3 = (s32[4]{0:T(128)S(1)}, s32[4]{0:T(128)}, u32[]{:S(2)}) copy-start(s32[4]{0:T(128)} %param.13) | copy-start | bytes 52
  20.1 89.5 %all-to-all-start.1 = ((bf16[16,128,896]{2,1,0:T(8,128)(2,1)}), bf16[16,128,896]{2,1,0:T(8,128)(2,1)}, u32[]{:S(2)}, u32[]{:S(2)}) async-start(bf16[16,128,896]{2,1,0:T(8,128)(2,1)} %broadcast_select_fusion), calls=%async_computation.1 | async-start | bytes 7340032 | tf_op jit(solution)/shard_map/all_to_all | solution.py:77
  27.0 82.3 %collective-permute-start = (bf16[63,2048]{1,0:T(8,128)(2,1)S(1)}, bf16[63,2048]{1,0:T(8,128)(2,1)S(1)}, u32[]{:S(2)}, u32[]{:S(2)}) collective-permute-start(bf16[63,2048]{1,0:T(8,128)(2,1)S(1)} %slice.13), channel_id=1, source_target_pairs={{1,0},{2,1},{3,2},{4,3},{5,4},{6,5},{7,6},{8,7},{9,8},{10,9},{11,1... | collective-permute-start | bytes 774152 | tf_op jit(solution)/shard_map/ppermute | solution.py:16
  112.5 2.0 %copy-start.4 = (bf16[896,2048]{1,0:T(8,128)(2,1)S(1)}, bf16[896,2048]{1,0:T(8,128)(2,1)}, u32[]{:S(2)}) copy-start(bf16[896,2048]{1,0:T(8,128)(2,1)} %param.9) | copy-start | bytes 11010052
  122.3 2.0 %copy-start.1 = (f32[4,16,64,256]{3,2,1,0:T(8,128)}, f32[4,16,64,256]{3,2,1,0:T(8,128)S(1)}, u32[]{:S(2)}) copy-start(f32[4,16,64,256]{3,2,1,0:T(8,128)S(1)} %fusion.3) | copy-start | bytes 12582916
  124.3 2.0 %copy-start.5 = (bf16[896,2048]{1,0:T(8,128)(2,1)S(1)}, bf16[896,2048]{1,0:T(8,128)(2,1)}, u32[]{:S(2)}) copy-start(bf16[896,2048]{1,0:T(8,128)(2,1)} %param.10) | copy-start | bytes 11010052
  147.5 8.8 %collective-permute-start.1 = (bf16[63,2048]{1,0:T(8,128)(2,1)S(1)}, bf16[63,2048]{1,0:T(8,128)(2,1)S(1)}, u32[]{:S(2)}, u32[]{:S(2)}) collective-permute-start(bf16[63,2048]{1,0:T(8,128)(2,1)S(1)} %slice.20), channel_id=1, source_target_pairs={{0,1},{1,2},{2,3},{3,4},{4,5},{5,6},{6,7},{7,8},{8,9},{9,10},{10,1... | collective-permute-start | bytes 774152 | tf_op jit(solution)/shard_map/ppermute | solution.py:16
where the time goes:
time: 158 us
  waiting for transfers between devices  85.4 us (54%)
  matrix products  23.1 us (15%)
  local copies, waits for them, and re-layouts  16.7 us (11%)
  starting transfers between devices  11.8 us (7%)
  other arithmetic  10.3 us (7%)
  blocking collectives  10.1 us (6%)
    ppermute x2, waiting for transfers between devices, from_behind(): lax.ppermute(value, axis, [(source, source + steps) for source in range(f...  85.4 us
    dot_general x1, matrix products, attend(): jnp.einsum('whqk,wkhd->wqhd', weights, value_heads, preferred_element_typ...  11.9 us
    all_to_all x1, blocking collectives, body(): lax.all_to_all(wanted.reshape(peer_count, capacity), 'seq', split_axis=0,...  10.1 us
    unnamed x17, local copies, waits for them, and re-layouts  9.37 us
    all_to_all x1, starting transfers between devices, body(): lax.all_to_all(picked, 'seq', split_axis=0, concat_axis=0, tiled=True)  6.81 us
    ppermute x2, starting transfers between devices, from_behind(): lax.ppermute(value, axis, [(source, source + steps) for source in range(f...  5 us
    dot_general x1, matrix products, project(): jnp.dot(normed, w_value, preferred_element_type=jnp.float32)  4.87 us
    dot_general x1, matrix products, project(): jnp.dot(normed, w_key, preferred_element_type=jnp.float32)  4.72 us
  transfers between devices with their start and end apart: 3, of which 2 were waited for; matrix products, arithmetic and copies ran while one was open for 1% of the time, Pallas kernels for 0%

commit v1 on v0

--- a/solution.py
+++ b/solution.py
@@ -20,13 +20,6 @@
     widened = tokens_in.astype(jnp.float32)
     factor = lax.rsqrt(jnp.mean(widened * widened, axis=-1, keepdims=True) + 1e-06)
     return (widened * factor).astype(jnp.bfloat16)
-
-
-def ranks_of(owner_rows):
-    count = owner_rows.shape[-1]
-    same = owner_rows[..., :, None] == owner_rows[..., None, :]
-    earlier = jnp.arange(count)[:, None] > jnp.arange(count)[None, :]
-    return jnp.sum(jnp.where(same & earlier, 1, 0), axis=-1).astype(jnp.int32)
 
 
 def project(chosen, w_key, w_value, span_count):
@@ -58,24 +51,12 @@
 
 
 def body(queries, neighbours, w_key, w_value, retrieval_owner, retrieval_slot, doc_starts):
-    peer_count = lax.axis_size("seq")
     span_count = doc_starts.shape[0]
     token_count = queries.shape[0]
     model_width = queries.shape[1]
-    request_count = 2 * span_count
-    capacity = (request_count + peer_count - 1) // peer_count
-    owners = retrieval_owner.reshape(-1)
-    slot_ids = retrieval_slot.reshape(-1)
-    destination = owners * capacity + ranks_of(owners)
-    targets = jnp.arange(peer_count * capacity, dtype=jnp.int32)
-    matches = destination[:, None] == targets[None, :]
-    wanted = jnp.sum(jnp.where(matches, slot_ids[:, None] + 1, 0), axis=0) - 1
-    asked_slot = lax.all_to_all(
-        wanted.reshape(peer_count, capacity), "seq", split_axis=0, concat_axis=0, tiled=True
-    ).reshape(-1)
-    picked = jnp.take(neighbours, jnp.maximum(asked_slot, 0), axis=0)
-    incoming = lax.all_to_all(picked, "seq", split_axis=0, concat_axis=0, tiled=True)
-    chosen = jnp.take(incoming, destination, axis=0)
+    stored = lax.all_gather(neighbours, "seq", axis=0, tiled=True)
+    wanted = (retrieval_owner * neighbours.shape[0] + retrieval_slot).reshape(-1)
+    chosen = jnp.take(stored, wanted, axis=0)
     key_rows, value_rows = project(chosen, w_key, w_value, span_count)
     tail_rows = from_behind(queries[: SPAN - 1], "seq", -1)
     query_rows = jnp.concatenate([queries[SPAN - 1 :], tail_rows], 0).reshape(

time: 158 us -> 134 us (0.85)
  the two profiles are of different devices: /device:TPU:18 before, /device:TPU:8 now
where the time goes in v1:
time: 134 us
  waiting for transfers between devices  70.9 us (53%)
  matrix products  23 us (17%)
  local copies, waits for them, and re-layouts  16 us (12%)
  between operations  13.6 us (10%)
  other arithmetic  5.64 us (4%)
  starting transfers between devices  4.91 us (4%)
    all_gather x1, waiting for transfers between devices, body(): stored = lax.all_gather(neighbours, 'seq', axis=0, tiled=True)  63.3 us
    dot_general x1, matrix products, attend(): jnp.einsum('whqk,wkhd->wqhd', weights, value_heads, preferred_element_typ...  11.9 us
    unnamed x10, local copies, waits for them, and re-layouts  8.53 us
    ppermute x2, waiting for transfers between devices, from_behind(): lax.ppermute(value, axis, [(source, source + steps) for source in range(f...  6.97 us
    ppermute x2, starting transfers between devices, from_behind(): lax.ppermute(value, axis, [(source, source + steps) for source in range(f...  4.91 us
    dot_general x1, matrix products, project(): jnp.dot(normed, w_value, preferred_element_type=jnp.float32)  4.87 us
    dot_general x1, matrix products, project(): jnp.dot(normed, w_key, preferred_element_type=jnp.float32)  4.69 us
    gather x1, local copies, waits for them, and re-layouts, body(): chosen = jnp.take(stored, wanted, axis=0)  3.93 us
  transfers between devices with their start and end apart: 3, of which 3 were waited for; matrix products, arithmetic and copies ran while one was open for 3% of the time, Pallas kernels for 0%

profile of v1, /device:TPU:8, one launch (start us, length us, event | category | flops | bytes accessed | tf_op | source)
XLA Modules:
  0.0 134.1 jit_solution(5957477104430302342)
XLA Ops:
  6.5 0.7 all-gather.2.cloned.1.call-update
  7.3 1.0 slice.13
  8.2 2.8 %collective-permute-start = (bf16[63,2048]{1,0:T(8,128)(2,1)S(1)}, bf16[63,2048]{1,0:T(8,128)(2,1)S(1)}, u32[]{:S(2)}, u32[]{:S(2)}) collective-permute-start(bf16[63,2048]{1,0:T(8,128)(2,1)S(1)} %slice.13), channel_id=1, source_target_pairs={{1,0},{2,1},{3,2},{4,3},{5,4},{6,5},{7,6},{8,7},{9,8},{10,9},{11,1... | collective-permute-start | bytes 774152 | tf_op jit(solution)/shard_map/ppermute | solution.py:16
  11.0 0.7 multiply_add_fusion
  11.7 0.1 copy.18
  11.8 0.1 reshape.114
  11.9 0.1 reshape.113
  12.1 1.3 slice.12
  13.4 0.7 compare_and_fusion.1
  14.1 0.8 collective-permute-done
  14.9 0.1 maximum_bitcast_fusion
  15.0 0.2 copy.24
  15.2 63.3 %all-gather.2.cloned.1.call-done = bf16[32,128,896]{2,1,0:T(8,128)(2,1)} async-done(((bf16[2,128,896]{2,1,0:T(8,128)(2,1)}), bf16[32,128,896]{2,1,0:T(8,128)(2,1)}) %all-gather.2.cloned.1.call-update) | async-done | bytes 7340048 | tf_op jit(solution)/shard_map/all_gather | solution.py:57
  78.5 3.9 %gather_fusion = bf16[8,128,896]{2,1,0:T(8,128)(2,1)S(1)} fusion(bf16[32,128,896]{2,1,0:T(8,128)(2,1)} %all-gather.2.cloned.1.call-done, s32[1024]{0:T(1024)S(1)} %pad_clamp_fusion), kind=kCustom, calls=%fused_computation | custom fusion | bytes 3670048 | tf_op jit(solution)/shard_map/jit(_take)/gather | solution.py:59
  82.4 0.6 multiply_reduce_fusion.1
  83.1 0.5 multiply_convert_fusion
  83.6 0.9 copy-done.1
  84.5 4.7 %convert_bitcast_fusion = bf16[128,8,16,128]{3,1,2,0:T(8,128)(2,1)S(1)} fusion(bf16[1024,896]{1,0:T(8,128)(2,1)S(1)} %multiply_convert_fusion, bf16[896,2048]{1,0:T(8,128)(2,1)S(1)} %copy-done.1), kind=kOutput, calls=%fused_computation.8 | convolution fusion | flops 3760193536 | bytes 9699328 | tf_op jit(solution)/shard_map/dot_general | solution.py:28
  89.2 1.4 %copy.25 = bf16[128,8,16,128]{3,2,1,0:T(8,128)(2,1)S(1)} copy(bf16[128,8,16,128]{3,1,2,0:T(8,128)(2,1)S(1)} %convert_bitcast_fusion) | data formatting | bytes 8388608
  90.6 1.6 %fusion.3 = f32[4,16,64,256]{3,2,1,0:T(8,128)S(1)} fusion(bf16[4,256,16,128]{3,2,1,0:T(8,128)(2,1)S(1)} %bitcast.33, bf16[4,64,16,128]{3,2,1,0:T(8,128)(2,1)S(1)} %bitcast.36), kind=kOutput, calls=%fused_computation.4 | convolution fusion | flops 268435456 | bytes 9437184 | tf_op jit(solution)/shard_map/wqhd,wkhd->whqk/dot_general | solution.py:41
  92.2 2.0 %copy-done = f32[4,16,64,256]{3,2,1,0:T(8,128)} copy-done((f32[4,16,64,256]{3,2,1,0:T(8,128)}, f32[4,16,64,256]{3,2,1,0:T(8,128)S(1)}, u32[]{:S(2)}) %copy-start) | copy-done | bytes 4194328
  94.1 1.6 %fusion.26 = f32[4,16,64]{2,1,0:T(8,128)S(1)} fusion(f32[4,16,64,256]{3,2,1,0:T(8,128)S(1)} %fusion.3), kind=kOutput, calls=%fused_computation.39 | output fusion | flops 4194559 | bytes 4210688 | tf_op jit(solution)/shard_map/sub | solution.py:46
  95.7 0.5 copy-done.2
  96.2 4.9 %convert_bitcast_fusion.1 = bf16[128,8,16,128]{3,1,2,0:T(8,128)(2,1)S(1)} fusion(bf16[1024,896]{1,0:T(8,128)(2,1)S(1)} %multiply_convert_fusion, bf16[896,2048]{1,0:T(8,128)(2,1)S(1)} %copy-done.2), kind=kOutput, calls=%fused_computation.9 | convolution fusion | flops 3760193536 | bytes 9699328 | tf_op jit(solution)/shard_map/dot_general | solution.py:29
  101.0 3.3 %copy.26 = bf16[128,8,16,128]{3,2,1,0:T(8,128)(2,1)} copy(bf16[128,8,16,128]{3,1,2,0:T(8,128)(2,1)S(1)} %convert_bitcast_fusion.1) | data formatting | bytes 8388608
  104.4 11.9 %fusion.13 = bf16[4,64,16,128]{3,1,2,0:T(8,128)(2,1)S(1)} fusion(bf16[4,256,16,128]{3,2,1,0:T(8,128)(2,1)} %bitcast.37, f32[4,16,64]{2,1,0:T(8,128)S(1)} %fusion.26, f32[4,16,64,256]{3,2,1,0:T(8,128)} %copy-done), kind=kOutput, calls=%fused_computation.18 | convolution fusion | flops 274206976 | bytes 9453568 | tf_op jit(solution)/shard_map/whqk,wkhd->wqhd/dot_general | solution.py:49
  116.3 0.7 copy.23
  117.0 0.3 copy.39
  117.3 2.2 %collective-permute-start.1 = (bf16[63,2048]{1,0:T(8,128)(2,1)S(1)}, bf16[63,2048]{1,0:T(8,128)(2,1)S(1)}, u32[]{:S(2)}, u32[]{:S(2)}) collective-permute-start(bf16[63,2048]{1,0:T(8,128)(2,1)S(1)} %slice.18), channel_id=1, source_target_pairs={{0,1},{1,2},{2,3},{3,4},{4,5},{5,6},{6,7},{7,8},{8,9},{9,10},{10,1... | collective-permute-start | bytes 774152 | tf_op jit(solution)/shard_map/ppermute | solution.py:16
  119.6 0.1 and.53
  119.7 6.2 %collective-permute-done.1 = bf16[63,2048]{1,0:T(8,128)(2,1)S(1)} collective-permute-done((bf16[63,2048]{1,0:T(8,128)(2,1)S(1)}, bf16[63,2048]{1,0:T(8,128)(2,1)S(1)}, u32[]{:S(2)}, u32[]{:S(2)}) %collective-permute-start.1) | collective-permute-done | bytes 258080 | tf_op jit(solution)/shard_map/ppermute | solution.py:16
  125.9 1.3 maximum_select_fusion
  (13 shorter events, 0.3 us)
Async XLA Ops:
  6.5 71.9 %all-gather.2.cloned.1.call-start = ((), (), s32[]{:S(2)}) async-start(), calls=%async_computation | async-start | bytes 7798784 | tf_op jit(solution)/shard_map/all_gather | solution.py:57
  8.2 6.6 %collective-permute-start = (bf16[63,2048]{1,0:T(8,128)(2,1)S(1)}, bf16[63,2048]{1,0:T(8,128)(2,1)S(1)}, u32[]{:S(2)}, u32[]{:S(2)}) collective-permute-start(bf16[63,2048]{1,0:T(8,128)(2,1)S(1)} %slice.13), channel_id=1, source_target_pairs={{1,0},{2,1},{3,2},{4,3},{5,4},{6,5},{7,6},{8,7},{9,8},{10,9},{11,1... | collective-permute-start | bytes 774152 | tf_op jit(solution)/shard_map/ppermute | solution.py:16
  82.4 2.0 %copy-start.1 = (bf16[896,2048]{1,0:T(8,128)(2,1)S(1)}, bf16[896,2048]{1,0:T(8,128)(2,1)}, u32[]{:S(2)}) copy-start(bf16[896,2048]{1,0:T(8,128)(2,1)} %param.9) | copy-start | bytes 11010052
  92.2 2.0 %copy-start = (f32[4,16,64,256]{3,2,1,0:T(8,128)}, f32[4,16,64,256]{3,2,1,0:T(8,128)S(1)}, u32[]{:S(2)}) copy-start(f32[4,16,64,256]{3,2,1,0:T(8,128)S(1)} %fusion.3) | copy-start | bytes 12582916
  94.1 2.0 %copy-start.2 = (bf16[896,2048]{1,0:T(8,128)(2,1)S(1)}, bf16[896,2048]{1,0:T(8,128)(2,1)}, u32[]{:S(2)}) copy-start(bf16[896,2048]{1,0:T(8,128)(2,1)} %param.10) | copy-start | bytes 11010052
  117.3 8.6 %collective-permute-start.1 = (bf16[63,2048]{1,0:T(8,128)(2,1)S(1)}, bf16[63,2048]{1,0:T(8,128)(2,1)S(1)}, u32[]{:S(2)}, u32[]{:S(2)}) collective-permute-start(bf16[63,2048]{1,0:T(8,128)(2,1)S(1)} %slice.18), channel_id=1, source_target_pairs={{0,1},{1,2},{2,3},{3,4},{4,5},{5,6},{6,7},{7,8},{8,9},{9,10},{10,1... | collective-permute-start | bytes 774152 | tf_op jit(solution)/shard_map/ppermute | solution.py:16
Sparse Core Ops, SparseCore 0:
  9.6 68.8 all-gather.1

commit v2 on v1

v2 whole, which is shorter than its diff:
```python
import functools
import math

import jax
import jax.numpy as jnp
from jax import lax
from jax.experimental import pallas as pl
from jax.experimental.pallas import tpu as pltpu
from jax.sharding import PartitionSpec as P

SPAN = 64
HEADS = 16
HEAD_DIM = 128
CHUNKS = 4
TAIL = 16
COLS = 256
UNROLL = 4


def ring_depth(mesh):
    devices = mesh.devices.reshape(mesh.shape["groups"], mesh.shape["seq"])[0]
    spots = [getattr(d, "coords", None) for d in devices[::2]]
    if any(s is None for s in spots) or len(spots) < 4:
        return 1
    spots = [tuple(s) for s in spots]
    apart = lambda a, b: {k for k in range(3) if a[k] != b[k]}
    return 2 if apart(spots[0], spots[1]).isdisjoint(apart(spots[0], spots[2])) else 1


def place_of(chip, chips, depth):
    if depth == 1:
        return chip
    far = chips // 2
    z, y = chip // 2, chip % 2
    return jnp.where(y == 0, z, 2 * far - 1 - z)


def chip_at(place, chips, depth):
    if depth == 1:
        return place
    far = chips // 2
    return jnp.where(place < far, 2 * place, 2 * (2 * far - 1 - place) + 1)


def kernel(
    n, depth,
    ids_s, ids_v, q_ref, nb_ref, wk_ref, wv_ref, out_ref,
    *scratch,
):
    gats = scratch[:CHUNKS]
    (w_ref, kv_ref, xn_ref, prev_v, prev_s,
     ring_recv, ring_send, pair_recv, pair_send, own_sem, w_sem, id_sem) = scratch[CHUNKS:]
    slots, length, width = nb_ref.shape
    rows = length // CHUNKS
    windows = kv_ref.shape[0]
    model = wk_ref.shape[1]
    requests = 2 * (windows - 1)
    chips = n // 2
    half = chips // 2

    me = lax.axis_index("seq")
    core = me % 2
    partner = me + 1 - 2 * core
    place = place_of(me // 2, chips, depth)

    def device_at(p):
        return chip_at((p + chips) % chips, chips, depth) * 2 + core

    right, left = device_at(place + 1), device_at(place - 1)
    nxt, prv = (me + 1) % n, (me + n - 1) % n

    w_copies = [
        pltpu.make_async_copy(wk_ref, w_ref.at[:, pl.ds(0, model)], w_sem.at[0]),
        pltpu.make_async_copy(wv_ref, w_ref.at[:, pl.ds(model, model)], w_sem.at[1]),
    ]
    own_copies = [
        pltpu.make_async_copy(
            nb_ref.at[:, pl.ds(g * rows, rows), :], gats[g].at[pl.ds(slots * me, slots)], own_sem.at[g]
        )
        for g in range(CHUNKS)
    ]

    barrier = pltpu.get_barrier_semaphore()
    for other in (left, right, partner, nxt, prv):
        pl.semaphore_signal(barrier, inc=1, device_id={"seq": other}, device_id_type=pl.DeviceIdType.MESH)
    pl.semaphore_wait(barrier, 5)

    id_copy = pltpu.make_async_remote_copy(
        src_ref=ids_v, dst_ref=prev_v, send_sem=id_sem.at[0], recv_sem=id_sem.at[1],
        device_id={"seq": nxt}, device_id_type=pl.DeviceIdType.MESH,
    )

    def ring_copy(g, d, way, slot):
        origin = device_at(place - (d - 1) if way == 0 else place + (d - 1))
        block = origin * slots + slot
        src = nb_ref.at[slot, pl.ds(g * rows, rows), :] if d == 1 else gats[g].at[block]
        return pltpu.make_async_remote_copy(
            src_ref=src, dst_ref=gats[g].at[block],
            send_sem=ring_send.at[g], recv_sem=ring_recv.at[g, d - 1, way, slot],
            device_id={"seq": right if way == 0 else left}, device_id_type=pl.DeviceIdType.MESH,
        )

    def pair_copy(g, d, way, slot):
        origin = device_at(place - d if way == 0 else place + d)
        block = origin * slots + slot
        src = nb_ref.at[slot, pl.ds(g * rows, rows), :] if d == 0 else gats[g].at[block]
        return pltpu.make_async_remote_copy(
            src_ref=src, dst_ref=gats[g].at[block],
            send_sem=pair_send.at[g], recv_sem=pair_recv.at[g],
            device_id={"seq": partner}, device_id_type=pl.DeviceIdType.MESH,
        )

    def items(d):
        return [(way, slot) for slot in range(slots) for way in range(2) if d < half or slot % 2 == way]

    def event(g, d):
        if d == 0:
            for way, slot in items(1):
                ring_copy(g, 1, way, slot).start()
            for slot in range(slots):
                pair_copy(g, 0, 0, slot).start()
            own_copies[g].start()
            return
        for way, slot in items(d):
            ring_copy(g, d, way, slot).wait_recv()
            if d < half and (way, slot) in items(d + 1):
                ring_copy(g, d + 1, way, slot).start()
            pair_copy(g, d, way, slot).start()

    def total(g, blocks, sem):
        part = gats[g].at[pl.ds(0, blocks)]
        return pltpu.make_async_copy(part, part, sem)

    def norm_piece(g):
        own_copies[g].wait()
        total(g, n * slots // 2, pair_recv.at[g]).wait()

        @pl.loop(0, requests + 2)
        def _(i):
            before = prev_s[0, requests - 2 + jnp.minimum(i, 1)]
            mine = ids_s[jnp.maximum(i - 2, 0)]
            x = gats[g][jnp.where(i < 2, before, mine)].astype(jnp.float32)
            factor = lax.rsqrt(jnp.mean(x * x, axis=-1, keepdims=True) + 1e-06)
            xn_ref[i] = (x * factor).astype(jnp.bfloat16)

    def proj_piece(g, part):
        xs = xn_ref.reshape(windows * 2 * rows, width)

        @pl.loop(0, model // COLS)
        def _(c):
            cols = pl.ds(pl.multiple_of(part * model + c * COLS, COLS), COLS)
            y = jnp.dot(xs[...], w_ref[:, cols], preferred_element_type=jnp.float32).astype(jnp.bfloat16)
            kv_ref[:, g * 2 * rows : (g + 1) * 2 * rows, cols] = y.reshape(windows, 2 * rows, COLS)

    stagger = max(half // 2, 1)
    order = sorted(
        ((stagger * g + d, g, d) for g in range(CHUNKS) for d in range(half + 1)),
    )
    id_copy.start()
    pending = []
    started = False
    for _, g, d in order:
        event(g, d)
        if not started:
            started = True
            for c in w_copies:
                c.start()
        if pending:
            pending.pop(0)()
        if g == 0 and d == half:
            id_copy.wait_recv()
            move = pltpu.make_async_copy(prev_v, prev_s, id_sem.at[2])
            move.start()
            move.wait()
            for c in w_copies:
                c.wait()
        if d == half:
            pending += [
                functools.partial(norm_piece, g),
                functools.partial(proj_piece, g, 0),
                functools.partial(proj_piece, g, 1),
            ]
    for piece in pending:
        piece()

    scale = 1.0 / math.sqrt(HEAD_DIM)

    def attend(w, start, count, h):
        cols = pl.ds(pl.multiple_of(h * HEAD_DIM, HEAD_DIM), HEAD_DIM)
        vcols = pl.ds(pl.multiple_of(model + h * HEAD_DIM, HEAD_DIM), HEAD_DIM)
        q = q_ref[pl.ds(start, count), cols]
        k = kv_ref[w, :, cols]
        v = kv_ref[w, :, vcols]
        s = lax.dot_general(q, k, (((1,), (1,)), ((), ())), preferred_element_type=jnp.float32) * scale
        p = jnp.exp(s - jnp.max(s, axis=-1, keepdims=True))
        p = (p / jnp.sum(p, axis=-1, keepdims=True)).astype(jnp.bfloat16)
        o = jnp.dot(p, v, preferred_element_type=jnp.float32)
        out_ref[pl.ds(start, count), cols] = o.astype(jnp.bfloat16)

    heads = model // HEAD_DIM

    @pl.loop(0, (windows - 1) * (heads // UNROLL))
    def _(t):
        w = t // (heads // UNROLL)
        for u in range(UNROLL):
            attend(w, pl.multiple_of(w * SPAN, SPAN), SPAN, (t % (heads // UNROLL)) * UNROLL + u)

    @pl.loop(0, heads // UNROLL)
    def _(t):
        for u in range(UNROLL):
            attend(windows - 1, (windows - 1) * SPAN, TAIL, t * UNROLL + u)

    id_copy.wait_send()
    for g in range(CHUNKS):
        total(g, (n - 2) * slots // 2, ring_send.at[g]).wait()
        total(g, n * slots // 2, pair_send.at[g]).wait()


def body(n, depth, queries, neighbours, w_key, w_value, retrieval_owner, retrieval_slot, doc_starts):
    span_count = doc_starts.shape[0]
    token_count, model = queries.shape
    slots, length, width = neighbours.shape
    windows = span_count + 1
    rows = length // CHUNKS
    chips = n // 2
    ids = (retrieval_owner * slots + retrieval_slot).reshape(-1)
    ids_wide = jnp.zeros((8, 128), jnp.int32).at[:, : 2 * span_count].set(ids[None, :])
    padded = jnp.pad(queries, ((1, TAIL - 1), (0, 0)))
    any_spec = pl.BlockSpec(memory_space=pl.ANY)
    vmem = pl.BlockSpec(memory_space=pltpu.VMEM)
    smem = pl.BlockSpec(memory_space=pltpu.SMEM)
    result = pl.pallas_call(
        functools.partial(kernel, n, depth),
        out_shape=jax.ShapeDtypeStruct((token_count + TAIL, model), jnp.bfloat16),
        in_specs=[smem, vmem, vmem, any_spec, any_spec, any_spec],
        out_specs=vmem,
        scratch_shapes=[pltpu.VMEM((n * slots, rows, width), jnp.bfloat16) for _ in range(CHUNKS)]
        + [
            pltpu.VMEM((width, 2 * model), jnp.bfloat16),
            pltpu.VMEM((windows, 2 * length, 2 * model), jnp.bfloat16),
            pltpu.VMEM((2 * windows, rows, width), jnp.bfloat16),
            pltpu.VMEM((8, 128), jnp.int32),
            pltpu.SMEM((8, 128), jnp.int32),
            pltpu.SemaphoreType.DMA((CHUNKS, chips // 2, 2, slots)),
            pltpu.SemaphoreType.DMA((CHUNKS,)),
            pltpu.SemaphoreType.DMA((CHUNKS,)),
            pltpu.SemaphoreType.DMA((CHUNKS,)),
            pltpu.SemaphoreType.DMA((CHUNKS,)),
            pltpu.SemaphoreType.DMA((2,)),
            pltpu.SemaphoreType.DMA((3,)),
        ],
        compiler_params=pltpu.CompilerParams(
            collective_id=0, has_side_effects=True, vmem_limit_bytes=60 * 1024 * 1024
        ),
    )(ids, ids_wide, padded, neighbours, w_key, w_value)
    attended = result[1 : token_count + 1]
    offsets = jnp.arange(SPAN)
    fresh_rows = (doc_starts[:, None] == 0) | (offsets[None, :] == SPAN - 1)
    opening = (
        (lax.axis_index("seq") == 0)
        & (jnp.arange(span_count)[:, None] == 0)
        & (offsets[None, :] < SPAN - 1)
    )
    kept_rows = (fresh_rows & jnp.logical_not(opening)).reshape(token_count)
    return jnp.where(kept_rows[:, None], attended, jnp.zeros((), jnp.bfloat16))


def solution(mesh):
    return jax.shard_map(
        functools.partial(body, mesh.shape["seq"], ring_depth(mesh)),
        mesh=mesh,
        in_specs=(
            P(("groups", "seq"), None),
            P(("groups", "seq"), None, None),
            P(),
            P(),
            P(("groups", "seq"), None),
            P(("groups", "seq"), None),
            P(("groups", "seq")),
        ),
        out_specs=P(("groups", "seq"), None),
        check_vma=False,
    )
```

time: 134 us -> 101 us (0.75)
  the two profiles are of different devices: /device:TPU:8 before, /device:TPU:0 now
where the time goes in v2:
time: 101 us
  Pallas kernels  93.2 us (92%)
  other arithmetic  4.63 us (5%)
  local copies, waits for them, and re-layouts  3.35 us (3%)
    pallas_call x1, Pallas kernels, body(): pl.pallas_call(functools.partial(kernel, n, depth), out_shape=jax.ShapeDt...  93.2 us
    select_n x1, other arithmetic, body(): return jnp.where(kept_rows[:, None], attended, jnp.zeros((), jnp.bfloat16))  2.56 us
    pad x1, local copies, waits for them, and re-layouts, body(): padded = jnp.pad(queries, ((1, TAIL - 1), (0, 0)))  2.48 us

profile of v2, /device:TPU:0, one launch (start us, length us, event | category | flops | bytes accessed | tf_op | source)
XLA Modules:
  0.0 101.2 jit_solution(13257374962417329794)
XLA Ops:
  0.0 0.7 multiply_add_fusion
  0.7 0.1 copy.9
  0.8 0.1 reshape.79.ids_s
  0.9 0.0 copy-start
  0.9 0.6 compare_reduce_fusion
  1.5 0.6 broadcast_select_fusion
  2.2 0.6 scatter.8.ids_v
  2.8 2.5 %pad.7.q_ref = bf16[272,2048]{1,0:T(8,128)(2,1)} pad(bf16[256,2048]{1,0:T(8,128)(2,1)} %param.9, bf16[]{:T(256)} %constant.42.clone.1), padding=1_15x0_0 | pad | bytes 2162690 | tf_op jit(solution)/shard_map/jit(_pad)/pad | solution.py:228
  5.3 0.0 copy-done
  5.3 0.0 copy-start.1
  5.3 93.2 %shard_map.73 = bf16[272,2048]{1,0:T(8,128)(2,1)} custom-call(s32[8]{0:T(128)} %copy-done, s32[8,128]{1,0:T(8,128)} %scatter.8.ids_v, bf16[272,2048]{1,0:T(8,128)(2,1)} %pad.7.q_ref, bf16[2,128,896]{2,1,0:T(8,128)(2,1)} %nb_ref.1, bf16[896,2048]{1,0:T(8,128)(2,1)} %wk_ref.1, bf16[896,2048]{1,0:T(8,128)(2,1)} %wv_ref.1), custom_call_target="tpu_custom_call" | custom-call | tf_op jit(solution)/shard_map/pallas_call | solution.py:232
  98.5 0.0 copy-done.1
  98.5 0.1 not_and_fusion
  98.6 0.1 and.50
  98.7 2.6 %slice_select_fusion = bf16[256,2048]{1,0:T(8,128)(2,1)} fusion(bf16[272,2048]{1,0:T(8,128)(2,1)} %shard_map.73, pred[256]{0:T(512)(128)(4,1)S(1)} %and.50), kind=kLoop, calls=%fused_computation | loop fusion | flops 524288 | bytes 2097408 | tf_op jit(solution)/shard_map/jit(_where)/select_n | solution.py:265
  (3 shorter events, 0.0 us)
Async XLA Ops:
  0.9 4.4 %copy-start = (s32[8]{0:T(128)}, s32[8]{0:T(128)S(1)}, u32[]{:S(2)}) copy-start(s32[8]{0:T(128)S(1)} %reshape.79.ids_s) | copy-start | bytes 100
  5.3 93.2 %copy-start.1 = (s32[4]{0:T(128)S(1)}, s32[4]{0:T(128)}, u32[]{:S(2)}) copy-start(s32[4]{0:T(128)} %param.15) | copy-start | bytes 52

commit v3 on v2

v3 whole, which is shorter than its diff:
```python
import functools
import math

import jax
import jax.numpy as jnp
from jax import lax
from jax.experimental import pallas as pl
from jax.experimental.pallas import tpu as pltpu
from jax.sharding import PartitionSpec as P

SPAN = 64
HEADS = 16
HEAD_DIM = 128
CHUNKS = 4
TAIL = 16
COLS = 256
UNROLL = 2
STAGGER = 1


def ring_depth(mesh):
    devices = mesh.devices.reshape(mesh.shape["groups"], mesh.shape["seq"])[0]
    spots = [getattr(d, "coords", None) for d in devices[::2]]
    if any(s is None for s in spots) or len(spots) < 4:
        return 1
    spots = [tuple(s) for s in spots]
    apart = lambda a, b: {k for k in range(3) if a[k] != b[k]}
    return 2 if apart(spots[0], spots[1]).isdisjoint(apart(spots[0], spots[2])) else 1


def place_of(chip, chips, depth):
    if depth == 1:
        return chip
    far = chips // 2
    z, y = chip // 2, chip % 2
    return jnp.where(y == 0, z, 2 * far - 1 - z)


def chip_at(place, chips, depth):
    if depth == 1:
        return place
    far = chips // 2
    return jnp.where(place < far, 2 * place, 2 * (2 * far - 1 - place) + 1)


def kernel(
    n, depth,
    owner_s, slot_s, doc_s, owner_v, slot_v, q_hbm, nb_ref, wk_ref, wv_ref, out_ref,
    *scratch,
):
    gats = scratch[:CHUNKS]
    (w_ref, kv_ref, xn_ref, q_raw, q_ref, keep_ref, prev_ov, prev_sv, prev_os, prev_ss,
     ring_recv, ring_send, pair_recv, pair_send, own_sem, w_sem, id_sem, q_sem) = scratch[CHUNKS:]
    slots, length, width = nb_ref.shape
    rows = length // CHUNKS
    windows = kv_ref.shape[0]
    spans = windows - 1
    model = wk_ref.shape[1]
    chips = n // 2
    half = chips // 2

    me = lax.axis_index("seq")
    core = me % 2
    partner = me + 1 - 2 * core
    place = place_of(me // 2, chips, depth)

    def device_at(p):
        return chip_at((p + chips) % chips, chips, depth) * 2 + core

    right, left = device_at(place + 1), device_at(place - 1)
    nxt, prv = (me + 1) % n, (me + n - 1) % n

    w_copies = [
        pltpu.make_async_copy(wk_ref, w_ref.at[:, pl.ds(0, model)], w_sem.at[0]),
        pltpu.make_async_copy(wv_ref, w_ref.at[:, pl.ds(model, model)], w_sem.at[1]),
    ]
    own_copies = [
        pltpu.make_async_copy(
            nb_ref.at[:, pl.ds(g * rows, rows), :], gats[g].at[pl.ds(slots * me, slots)], own_sem.at[g]
        )
        for g in range(CHUNKS)
    ]

    q_copy = pltpu.make_async_copy(q_hbm, q_raw, q_sem)

    barrier = pltpu.get_barrier_semaphore()
    for other in (left, right, partner, nxt, prv):
        pl.semaphore_signal(barrier, inc=1, device_id={"seq": other}, device_id_type=pl.DeviceIdType.MESH)
    pl.semaphore_wait(barrier, 5)

    id_copies = [
        pltpu.make_async_remote_copy(
            src_ref=src, dst_ref=dst, send_sem=id_sem.at[k, 0], recv_sem=id_sem.at[k, 1],
            device_id={"seq": nxt}, device_id_type=pl.DeviceIdType.MESH,
        )
        for k, (src, dst) in enumerate(((owner_v, prev_ov), (slot_v, prev_sv)))
    ]
    id_moves = [
        pltpu.make_async_copy(prev_ov, prev_os, id_sem.at[0, 2]),
        pltpu.make_async_copy(prev_sv, prev_ss, id_sem.at[1, 2]),
    ]

    def share(g, origin, slot, count, own):
        block = origin * slots + slot
        if own:
            return nb_ref.at[pl.ds(slot, count), pl.ds(g * rows, rows), :], gats[g].at[pl.ds(block, count)]
        return gats[g].at[pl.ds(block, count)], gats[g].at[pl.ds(block, count)]

    def ring_copy(g, d, way):
        origin = device_at(place - (d - 1) if way == 0 else place + (d - 1))
        slot, count = (0, slots) if d < half else (way * slots // 2, slots // 2)
        src, dst = share(g, origin, slot, count, d == 1)
        return pltpu.make_async_remote_copy(
            src_ref=src, dst_ref=dst,
            send_sem=ring_send.at[g], recv_sem=ring_recv.at[g, d - 1, way],
            device_id={"seq": right if way == 0 else left}, device_id_type=pl.DeviceIdType.MESH,
        )

    def pair_copy(g, d, way):
        origin = device_at(place - d if way == 0 else place + d)
        slot, count = (0, slots) if d < half else (way * slots // 2, slots // 2)
        src, dst = share(g, origin, slot, count, d == 0)
        return pltpu.make_async_remote_copy(
            src_ref=src, dst_ref=dst,
            send_sem=pair_send.at[g], recv_sem=pair_recv.at[g],
            device_id={"seq": partner}, device_id_type=pl.DeviceIdType.MESH,
        )

    def event(g, d):
        if d == 0:
            for way in range(2):
                ring_copy(g, 1, way).start()
            pair_copy(g, 0, 0).start()
            own_copies[g].start()
            return
        for way in range(2):
            ring_copy(g, d, way).wait_recv()
            if d < half:
                ring_copy(g, d + 1, way).start()
            pair_copy(g, d, way).start()

    def total(g, blocks, sem):
        part = gats[g].at[pl.ds(0, blocks)]
        return pltpu.make_async_copy(part, part, sem)

    def norm_piece(g):
        own_copies[g].wait()
        total(g, n * slots // 2, pair_recv.at[g]).wait()

        @pl.loop(0, 2 * windows)
        def _(i):
            span, j = jnp.maximum(i // 2 - 1, 0), i % 2
            before = prev_os[spans - 1, j] * slots + prev_ss[spans - 1, j]
            mine = owner_s[span, j] * slots + slot_s[span, j]
            x = gats[g][jnp.where(i < 2, before, mine)].astype(jnp.float32)
            factor = lax.rsqrt(jnp.mean(x * x, axis=-1, keepdims=True) + 1e-06)
            xn_ref[i] = (x * factor).astype(jnp.bfloat16)

    def proj_piece(g, part):
        xs = xn_ref.reshape(windows * 2 * rows, width)

        @pl.loop(0, model // COLS)
        def _(c):
            cols = pl.ds(pl.multiple_of(part * model + c * COLS, COLS), COLS)
            y = jnp.dot(xs[...], w_ref[:, cols], preferred_element_type=jnp.float32).astype(jnp.bfloat16)
            kv_ref[:, g * 2 * rows : (g + 1) * 2 * rows, cols] = y.reshape(windows, 2 * rows, COLS)

    def shift_piece():
        q_copy.wait()

        @pl.loop(0, model // COLS)
        def _(c):
            cols = pl.ds(pl.multiple_of(c * COLS, COLS), COLS)
            q_ref[:, cols] = pltpu.roll(q_raw[:, cols].astype(jnp.float32), 1, 0).astype(jnp.bfloat16)

        at = lax.broadcasted_iota(jnp.int32, (SPAN, HEAD_DIM), 0)
        for c in range(spans):
            open_row = (1 - doc_s[c]).astype(jnp.float32)
            if c == 0:
                open_row = jnp.where(me == 0, 0.0, open_row)
            keep_ref[c * SPAN : (c + 1) * SPAN, :] = jnp.where(at == SPAN - 1, 1.0, open_row)

    def id_piece():
        for copy, move in zip(id_copies, id_moves):
            copy.wait_recv()
            move.start()
        for move in id_moves:
            move.wait()
        for c in w_copies:
            c.wait()

    order = sorted(
        ((STAGGER * g + d, g, d) for g in range(CHUNKS) for d in range(half + 1)),
    )
    for copy in id_copies:
        copy.start()
    pending = []
    for at, (_, g, d) in enumerate(order):
        event(g, d)
        if at == 0:
            q_copy.start()
            for c in w_copies:
                c.start()
            pending = [shift_piece, id_piece]
        elif pending:
            pending.pop(0)()
        if d == half:
            pending += [
                functools.partial(norm_piece, g),
                functools.partial(proj_piece, g, 0),
                functools.partial(proj_piece, g, 1),
            ]
    for piece in pending:
        piece()

    scale = math.log2(math.e) / math.sqrt(HEAD_DIM)
    starts = [(w, w * SPAN, SPAN) for w in range(spans)] + [(spans, 0, TAIL)]

    @pl.loop(0, model // HEAD_DIM // UNROLL)
    def _(t):
        heads = [t * UNROLL + u for u in range(UNROLL)]
        cols = [pl.ds(pl.multiple_of(h * HEAD_DIM, HEAD_DIM), HEAD_DIM) for h in heads]
        vcols = [pl.ds(pl.multiple_of(model + h * HEAD_DIM, HEAD_DIM), HEAD_DIM) for h in heads]
        each = [(u, w, start, count) for u in range(UNROLL) for w, start, count in starts]
        s = [
            lax.dot_general(
                q_ref[start : start + count, cols[u]], kv_ref[w, :, cols[u]],
                (((1,), (1,)), ((), ())), preferred_element_type=jnp.float32,
            )
            for u, w, start, count in each
        ]
        top = [jnp.max(x, axis=-1, keepdims=True) for x in s]
        p = [jnp.exp2((x - m) * scale) for x, m in zip(s, top)]
        o = [
            jnp.dot(x.astype(jnp.bfloat16), kv_ref[w, :, vcols[u]], preferred_element_type=jnp.float32)
            for x, (u, w, _, _) in zip(p, each)
        ]
        o = [x / jnp.sum(y, axis=-1, keepdims=True) for x, y in zip(o, p)]
        first = lax.broadcasted_iota(jnp.int32, (TAIL, HEAD_DIM), 0) == 0
        for u in range(UNROLL):
            parts = o[u * windows : (u + 1) * windows]
            head = jnp.where(first, parts[-1], parts[0][:TAIL])
            full = jnp.concatenate([head, parts[0][TAIL:]] + parts[1:-1], 0)
            full = pltpu.roll(full, spans * SPAN - 1, 0)
            out_ref[:, cols[u]] = jnp.where(keep_ref[...] > 0.5, full, 0.0).astype(jnp.bfloat16)

    for copy in id_copies:
        copy.wait_send()
    for g in range(CHUNKS):
        total(g, (n - 2) * slots // 2, ring_send.at[g]).wait()
        total(g, n * slots // 2, pair_send.at[g]).wait()


def body(n, depth, queries, neighbours, w_key, w_value, retrieval_owner, retrieval_slot, doc_starts):
    span_count = doc_starts.shape[0]
    token_count, model = queries.shape
    slots, length, width = neighbours.shape
    windows = span_count + 1
    rows = length // CHUNKS
    chips = n // 2
    any_spec = pl.BlockSpec(memory_space=pl.ANY)
    vmem = pl.BlockSpec(memory_space=pltpu.VMEM)
    smem = pl.BlockSpec(memory_space=pltpu.SMEM)
    return pl.pallas_call(
        functools.partial(kernel, n, depth),
        out_shape=jax.ShapeDtypeStruct((token_count, model), jnp.bfloat16),
        in_specs=[smem, smem, smem, vmem, vmem] + [any_spec] * 4,
        out_specs=vmem,
        scratch_shapes=[pltpu.VMEM((n * slots, rows, width), jnp.bfloat16) for _ in range(CHUNKS)]
        + [
            pltpu.VMEM((width, 2 * model), jnp.bfloat16),
            pltpu.VMEM((windows, 2 * length, 2 * model), jnp.bfloat16),
            pltpu.VMEM((2 * windows, rows, width), jnp.bfloat16),
            pltpu.VMEM((token_count, model), jnp.bfloat16),
            pltpu.VMEM((token_count, model), jnp.bfloat16),
            pltpu.VMEM((token_count, HEAD_DIM), jnp.float32),
            pltpu.VMEM(retrieval_owner.shape, jnp.int32),
            pltpu.VMEM(retrieval_slot.shape, jnp.int32),
            pltpu.SMEM(retrieval_owner.shape, jnp.int32),
            pltpu.SMEM(retrieval_slot.shape, jnp.int32),
            pltpu.SemaphoreType.DMA((CHUNKS, chips // 2, 2)),
            pltpu.SemaphoreType.DMA((CHUNKS,)),
            pltpu.SemaphoreType.DMA((CHUNKS,)),
            pltpu.SemaphoreType.DMA((CHUNKS,)),
            pltpu.SemaphoreType.DMA((CHUNKS,)),
            pltpu.SemaphoreType.DMA((2,)),
            pltpu.SemaphoreType.DMA((2, 3)),
            pltpu.SemaphoreType.DMA,
        ],
        compiler_params=pltpu.CompilerParams(
            collective_id=0, has_side_effects=True, vmem_limit_bytes=60 * 1024 * 1024
        ),
    )(
        retrieval_owner, retrieval_slot, doc_starts, retrieval_owner, retrieval_slot,
        queries, neighbours, w_key, w_value,
    )


def solution(mesh):
    return jax.shard_map(
        functools.partial(body, mesh.shape["seq"], ring_depth(mesh)),
        mesh=mesh,
        in_specs=(
            P(("groups", "seq"), None),
            P(("groups", "seq"), None, None),
            P(),
            P(),
            P(("groups", "seq"), None),
            P(("groups", "seq"), None),
            P(("groups", "seq")),
        ),
        out_specs=P(("groups", "seq"), None),
        check_vma=False,
    )
```

time: 101 us -> 72.3 us (0.72)
  Pallas kernels: 93.2 us -> 67.1 us
  other arithmetic: 4.63 us -> 0 us
  local copies, waits for them, and re-layouts: 3.35 us -> 4.99 us
    pallas_call x1, Pallas kernels: 93.2 us -> 67.1 us  [body(): pl.pallas_call(functools.partial(kernel, n, depth), out_shape=jax.ShapeDt...]
    unnamed x4 -> x3, local copies, waits for them, and re-layouts: 0.01 us -> 4.99 us
    select_n x1 -> x0, other arithmetic: 2.56 us -> none  [body(): return jnp.where(kept_rows[:, None], attended, jnp.zeros((), jnp.bfloat16))]
    pad x1 -> x0, local copies, waits for them, and re-layouts: 2.48 us -> none  [body(): padded = jnp.pad(queries, ((1, TAIL - 1), (0, 0)))]
    another operation x2 -> x0, other arithmetic: 1.29 us -> none
where the time goes in v3:
time: 72.3 us; the launch traced here: 72.1 us
  Pallas kernels  67.1 us (93%)
  local copies, waits for them, and re-layouts  4.99 us (7%)
    pallas_call x1, Pallas kernels, body(): pl.pallas_call(functools.partial(kernel, n, depth), out_shape=jax.ShapeDt...  67.1 us
    unnamed x3, local copies, waits for them, and re-layouts  4.99 us

profile of v3, /device:TPU:0, one launch (start us, length us, event | category | flops | bytes accessed | tf_op | source)
XLA Modules:
  0.0 72.1 jit_solution(11448451275132403411)
XLA Ops:
  0.0 1.3 %copy.8.owner_s.owner_v = s32[4,2]{1,0:T(4,128)} copy(s32[4,2]{0,1:T(2,128)} %param.11) | data formatting | bytes 64 | tf_op args[4]
  1.3 1.3 %copy.9.slot_s.slot_v = s32[4,2]{1,0:T(4,128)} copy(s32[4,2]{0,1:T(2,128)} %param.12) | data formatting | bytes 64 | tf_op args[5]
  2.7 67.1 %shard_map.73 = bf16[256,2048]{1,0:T(8,128)(2,1)} custom-call(s32[4,2]{1,0:T(4,128)} %copy.8.owner_s.owner_v, s32[4,2]{1,0:T(4,128)} %copy.9.slot_s.slot_v, s32[4]{0:T(128)} %doc_s.1, s32[4,2]{1,0:T(4,128)} %copy.8.owner_s.owner_v, s32[4,2]{1,0:T(4,128)} %copy.9.slot_s.slot_v, bf16[256,2048]{1,0:T(8,128)(2,1)} %q_hbm.1, bf16[2,128,896]{2,1,0:T(8,128)(2,1)} %nb_ref.1, ...), custom_call_target="tpu_custom_call" | custom-call | tf_op jit(solution)/shard_map/pallas_call | solution.py:264
  69.7 2.3 %copy.13 = bf16[256,2048]{1,0:T(8,128)(2,1)} copy(bf16[256,2048]{1,0:T(8,128)(2,1)} %shard_map.73) | data formatting | bytes 2097152

commit v4 on v3

--- a/solution.py
+++ b/solution.py
@@ -13,8 +13,8 @@
 HEAD_DIM = 128
 CHUNKS = 4
 TAIL = 16
-COLS = 256
-UNROLL = 2
+COLS = 1024
+UNROLL = 4
 STAGGER = 1
 
 
@@ -150,8 +150,8 @@
         @pl.loop(0, 2 * windows)
         def _(i):
             span, j = jnp.maximum(i // 2 - 1, 0), i % 2
-            before = prev_os[spans - 1, j] * slots + prev_ss[spans - 1, j]
-            mine = owner_s[span, j] * slots + slot_s[span, j]
+            before = prev_os[j, spans - 1] * slots + prev_ss[j, spans - 1]
+            mine = owner_s[j, span] * slots + slot_s[j, span]
             x = gats[g][jnp.where(i < 2, before, mine)].astype(jnp.float32)
             factor = lax.rsqrt(jnp.mean(x * x, axis=-1, keepdims=True) + 1e-06)
             xn_ref[i] = (x * factor).astype(jnp.bfloat16)
@@ -258,6 +258,7 @@
     windows = span_count + 1
     rows = length // CHUNKS
     chips = n // 2
+    owner_rows, slot_rows = retrieval_owner.T, retrieval_slot.T
     any_spec = pl.BlockSpec(memory_space=pl.ANY)
     vmem = pl.BlockSpec(memory_space=pltpu.VMEM)
     smem = pl.BlockSpec(memory_space=pltpu.SMEM)
@@ -274,10 +275,10 @@
             pltpu.VMEM((token_count, model), jnp.bfloat16),
             pltpu.VMEM((token_count, model), jnp.bfloat16),
             pltpu.VMEM((token_count, HEAD_DIM), jnp.float32),
-            pltpu.VMEM(retrieval_owner.shape, jnp.int32),
-            pltpu.VMEM(retrieval_slot.shape, jnp.int32),
-            pltpu.SMEM(retrieval_owner.shape, jnp.int32),
-            pltpu.SMEM(retrieval_slot.shape, jnp.int32),
+            pltpu.VMEM(owner_rows.shape, jnp.int32),
+            pltpu.VMEM(slot_rows.shape, jnp.int32),
+            pltpu.SMEM(owner_rows.shape, jnp.int32),
+            pltpu.SMEM(slot_rows.shape, jnp.int32),
             pltpu.SemaphoreType.DMA((CHUNKS, chips // 2, 2)),
             pltpu.SemaphoreType.DMA((CHUNKS,)),
             pltpu.SemaphoreType.DMA((CHUNKS,)),
@@ -291,7 +292,7 @@
             collective_id=0, has_side_effects=True, vmem_limit_bytes=60 * 1024 * 1024
         ),
     )(
-        retrieval_owner, retrieval_slot, doc_starts, retrieval_owner, retrieval_slot,
+        owner_rows, slot_rows, doc_starts, owner_rows, slot_rows,
         queries, neighbours, w_key, w_value,
     )
 

time: 72.3 us -> 62.1 us (0.86)
  Pallas kernels: 67.1 us -> 59.6 us
  local copies, waits for them, and re-layouts: 4.99 us -> 2.3 us
    pallas_call x1, Pallas kernels: 67.1 us -> 59.6 us  [body(): pl.pallas_call(functools.partial(kernel, n, depth), out_shape=jax.ShapeDt...]
    unnamed x3 -> x1, local copies, waits for them, and re-layouts: 4.99 us -> 2.3 us
where the time goes in v4:
time: 62.1 us; the launch traced here: 61.9 us
  Pallas kernels  59.6 us (96%)
  local copies, waits for them, and re-layouts  2.3 us (4%)
    pallas_call x1, Pallas kernels, body(): pl.pallas_call(functools.partial(kernel, n, depth), out_shape=jax.ShapeDt...  59.6 us
    unnamed x1, local copies, waits for them, and re-layouts  2.3 us

profile of v4, /device:TPU:0, one launch (start us, length us, event | category | flops | bytes accessed | tf_op | source)
XLA Modules:
  0.0 61.9 jit_solution(13736524146206334797)
XLA Ops:
  0.0 59.6 %shard_map.73 = bf16[256,2048]{1,0:T(8,128)(2,1)} custom-call(s32[2,4]{1,0:T(2,128)} %bitcast.2, s32[2,4]{1,0:T(2,128)} %bitcast.4, s32[4]{0:T(128)} %doc_s.1, s32[2,4]{1,0:T(2,128)} %bitcast.3, s32[2,4]{1,0:T(2,128)} %bitcast.5, bf16[256,2048]{1,0:T(8,128)(2,1)} %q_hbm.1, bf16[2,128,896]{2,1,0:T(8,128)(2,1)} %nb_ref.1, bf16[896,2048]{1,0:T(8,128)(2,1)} %wk_ref.1, ...), custom_call_target="tpu_custom_call" | custom-call | tf_op jit(solution)/shard_map/pallas_call | solution.py:265
  59.6 2.3 %copy.9 = bf16[256,2048]{1,0:T(8,128)(2,1)} copy(bf16[256,2048]{1,0:T(8,128)(2,1)} %shard_map.73) | data formatting | bytes 2097152
